TPU v7x, 32 devices: a whole 2x2x4 slice. The times are simulated.
32 devices in a mesh: ctx: 16 (over z, x, core), head: 2 (over y).
Axes of the slice: x: 2, y: 2, z: 4, core: 2. Of those that a mesh axis runs over, the one named last changes fastest.
Arguments:
- features: float32 [4096, 8192], P(('ctx', 'head')), may hold values from -200 to 200
- state_write: float32 [4096, 1024], P(('ctx', 'head')), may hold values from -6 to 6
- state_read: float32 [4096, 1024], P(('ctx', 'head')), may hold values from -6 to 6
- log_decay: float32 [4096, 128], P(('ctx', 'head')), may hold values from -0.6932 to 0, as said below
- conv_features: float32 [4, 8192], replicated, may hold values from -3 to 3
- conv_write: float32 [4, 1024], replicated, may hold values from -3 to 3
- conv_read: float32 [4, 1024], replicated, may hold values from -3 to 3
- norm_gain: float32 [8192], P('head'), may hold values from 0.5 to 1.5
Outputs:
- normed_head_outputs: float32 [4096, 8192], P('ctx', 'head')
Inputs may be any that keep to these rules, and one draw needn't show every extreme that they name: `log_decay`: strictly negative.
All inputs are finite; a program needn't handle non-finite values.
Results may differ from a plain program's by a relative error of at most 0.00029.
Values sent between devices are 32-bit elements; how exact they have to be, the bound alone decides.
A program may use at most 128 MiB of HBM per device.

v0:
```python
import jax
import jax.numpy as jnp
from jax import lax
from jax.sharding import PartitionSpec as P

H = 128
P_SIZE = 64
N = 128
G = 8
BLOCK = 256
highest = lax.Precision.HIGHEST
eps_norm = 1e-05


def passed_along(value, axis, steps):
    count = lax.axis_size(axis)
    leading, last = (max(0, -steps), min(count, count - steps))
    return lax.ppermute(value, axis, [(source, source + steps) for source in range(leading, last)])


def causal_conv(tokens, leading, weight):
    tap_count = weight.shape[0]
    padded = jnp.concatenate([leading, tokens], 0)
    extent = tokens.shape[0]
    summed = weight[0] * padded[0:extent]
    for displacement in range(1, tap_count):
        summed = summed + weight[displacement] * padded[displacement : displacement + extent]
    return jax.nn.silu(summed)


def block_pass(carried_state, blocked):
    inputs_act, writes_act, reads_act, decays = blocked
    cumulative = jnp.cumsum(decays, 0)
    extent = decays.shape[0]
    target = lax.broadcasted_iota(jnp.int32, (extent, extent), 0)
    source = lax.broadcasted_iota(jnp.int32, (extent, extent), 1)
    strictly_past = target >= source
    along = jnp.transpose(cumulative, (1, 2, 0))
    spacing = jnp.where(strictly_past, along[..., :, None] - along[..., None, :], 0.0)
    damping = jnp.where(strictly_past, jnp.exp(spacing), 0.0)
    scores = jnp.einsum("tgn,sgn->gts", reads_act, writes_act, precision=highest)
    within_range = jnp.einsum(
        "ghts,sghp->tghp", scores[:, None] * damping, inputs_act, precision=highest
    )
    entering = (
        jnp.einsum("tgn,ghpn->tghp", reads_act, carried_state, precision=highest)
        * jnp.exp(cumulative)[..., None]
    )
    remaining = jnp.exp(cumulative[-1] - cumulative)
    new_state = jnp.exp(cumulative[-1])[..., None, None] * carried_state + jnp.einsum(
        "sgh,sghp,sgn->ghpn", remaining, inputs_act, writes_act, precision=highest
    )
    return (new_state, within_range + entering)


def split_rim(edges, first_width, second_width):
    return (
        edges[:, :first_width],
        edges[:, first_width : first_width + second_width],
        edges[:, first_width + second_width :],
    )


def shards(
    features, state_write, state_read, log_decay, conv_features, conv_write, conv_read, norm_gain
):
    tap_count = conv_features.shape[0]
    head_count = lax.axis_size("head")
    local_heads = H // head_count
    groups_here = G // head_count
    per_group = H // G
    moving = (features, state_write, state_read)
    inputs_act, writes_act, reads_act, decays = (
        lax.all_to_all(moving[0], "head", split_axis=1, concat_axis=0, tiled=True),
        lax.all_to_all(moving[1], "head", split_axis=1, concat_axis=0, tiled=True),
        lax.all_to_all(moving[2], "head", split_axis=1, concat_axis=0, tiled=True),
        lax.all_to_all(log_decay, "head", split_axis=1, concat_axis=0, tiled=True),
    )
    rim = jnp.concatenate(
        [
            inputs_act[-(tap_count - 1) :],
            writes_act[-(tap_count - 1) :],
            reads_act[-(tap_count - 1) :],
        ],
        1,
    )
    edges = passed_along(rim, "ctx", 1)
    lead_inputs, lead_writes, lead_reads = split_rim(
        edges, inputs_act.shape[1], writes_act.shape[1]
    )
    position = lax.axis_index("head")
    input_width = inputs_act.shape[1]
    state_width = writes_act.shape[1]
    inputs_act = causal_conv(
        inputs_act,
        lead_inputs,
        lax.dynamic_slice_in_dim(conv_features, position * input_width, input_width, 1),
    )
    writes_act = causal_conv(
        writes_act,
        lead_writes,
        lax.dynamic_slice_in_dim(conv_write, position * state_width, state_width, 1),
    )
    reads_act = causal_conv(
        reads_act,
        lead_reads,
        lax.dynamic_slice_in_dim(conv_read, position * state_width, state_width, 1),
    )
    length = inputs_act.shape[0]
    blocks = length // BLOCK
    blocked = (
        inputs_act.reshape(blocks, BLOCK, groups_here, per_group, P_SIZE),
        writes_act.reshape(blocks, BLOCK, groups_here, N),
        reads_act.reshape(blocks, BLOCK, groups_here, N),
        decays.reshape(blocks, BLOCK, groups_here, per_group),
    )
    initial = jnp.zeros((groups_here, per_group, P_SIZE, N), jnp.float32)
    final_state, partial_value = lax.scan(block_pass, initial, blocked)
    within = partial_value.reshape(length, groups_here, per_group, P_SIZE)
    decay_groups = decays.reshape(length, groups_here, per_group)
    segment_log = jnp.sum(decay_groups, 0)
    flattened = final_state.reshape(1, local_heads, P_SIZE * N)
    pieces = lax.all_to_all(flattened, "ctx", split_axis=2, concat_axis=0, tiled=True)
    totals = lax.all_gather(segment_log.reshape(1, local_heads), "ctx", axis=0, tiled=True)
    running = jnp.cumsum(totals, 0)
    segments = totals.shape[0]
    target = lax.broadcasted_iota(jnp.int32, (segments, segments), 0)
    source = lax.broadcasted_iota(jnp.int32, (segments, segments), 1)
    before = (source < target)[..., None]
    spacing = jnp.where(before, (running - totals)[:, None, :] - running[None, :, :], 0.0)
    weight = jnp.where(before, jnp.exp(spacing), 0.0)
    prefix = jnp.einsum("cdh,dhq->chq", weight, pieces, precision=highest)
    returned = lax.all_to_all(prefix, "ctx", split_axis=0, concat_axis=2, tiled=True)
    incoming = returned.reshape(groups_here, per_group, P_SIZE, N)
    rising = jnp.exp(jnp.cumsum(decay_groups, 0))
    carried = (
        jnp.einsum(
            "tgn,ghpn->tghp", reads_act.reshape(length, groups_here, N), incoming, precision=highest
        )
        * rising[..., None]
    )
    mixed = (within + carried).reshape(length, groups_here, per_group * P_SIZE)
    inverse = lax.rsqrt(jnp.mean(mixed * mixed, -1, keepdims=True) + eps_norm)
    return (mixed * inverse).reshape(length, local_heads * P_SIZE) * norm_gain


def solution(mesh):
    return jax.shard_map(
        shards,
        mesh=mesh,
        in_specs=(
            P(("ctx", "head"), None),
            P(("ctx", "head"), None),
            P(("ctx", "head"), None),
            P(("ctx", "head"), None),
            P(),
            P(),
            P(),
            P("head"),
        ),
        out_specs=P("ctx", "head"),
        check_vma=False,
    )
```

profile of v0, /device:TPU:11, one launch (start us, length us, event | category | flops | bytes accessed | tf_op | source)
XLA Modules:
  0.0 362.2 jit_solution(3611909566729080655)
XLA Ops:
  0.0 1.6 copy.62
  1.6 3.3 all-to-all-start.3
  4.9 2.0 copy.53
  6.9 0.9 all-to-all-done.3
  7.8 3.5 all-to-all-start.1
  11.3 2.0 copy.55
  13.3 4.2 %all-to-all-done.1 = f32[128,2,512]{0,2,1:T(8,128)S(1)} async-done(((f32[128,2,512]{0,2,1:T(8,128)}), f32[128,2,512]{0,2,1:T(8,128)S(1)}, u32[]{:S(2)}, u32[]{:S(2)}) %all-to-all-start.1) | async-done | bytes 524320 | tf_op jit(solution)/shard_map/all_to_all | solution.py:75
  17.5 3.5 all-to-all-start.2
  21.0 5.6 %copy.51 = f32[128,8192]{0,1:T(8,128)} copy(f32[128,8192]{1,0:T(8,128)} %param.8) | data formatting | bytes 8388608 | tf_op args[0]
  26.6 5.8 %all-to-all-start = ((f32[128,2,4096]{0,2,1:T(8,128)}), f32[128,2,4096]{0,2,1:T(8,128)}, u32[]{:S(2)}, u32[]{:S(2)}) async-start(f32[128,2,4096]{0,2,1:T(8,128)} %bitcast.110), calls=%async_computation | async-start | bytes 8388608 | tf_op jit(solution)/shard_map/all_to_all | solution.py:74
  32.9 2.3 reduce-window.12
  36.2 40.1 %all-to-all-done = f32[128,2,4096]{0,2,1:T(8,128)} async-done(((f32[128,2,4096]{0,2,1:T(8,128)}), f32[128,2,4096]{0,2,1:T(8,128)}, u32[]{:S(2)}, u32[]{:S(2)}) %all-to-all-start) | async-done | bytes 4194336 | tf_op jit(solution)/shard_map/all_to_all | solution.py:74
  76.2 5.6 %copy.52 = f32[2,128,4096]{2,1,0:T(8,128)} copy(f32[2,128,4096]{1,2,0:T(8,128)} %bitcast.2) | data formatting | bytes 8388608 | tf_op jit(solution)/shard_map/all_to_all | solution.py:74
  81.8 0.9 slice.124
  82.8 8.1 %collective-permute-start = (f32[3,5120]{1,0:T(4,128)S(1)}, f32[3,5120]{1,0:T(4,128)S(1)}, u32[]{:S(2)}, u32[]{:S(2)}) collective-permute-start(f32[3,5120]{1,0:T(4,128)S(1)} %pad_maximum_fusion.3), channel_id=1, source_target_pairs={{0,2},{2,4},{4,6},{6,8},{8,10},{10,12},{12,14},{14,16},{16,18},{18... | collective-permute-start | bytes 184328 | tf_op jit(solution)/shard_map/ppermute | solution.py:18
  90.9 0.9 collective-permute-done
  91.8 0.3 divide_multiply_fusion.1
  92.4 8.9 %divide_multiply_fusion = f32[256,4096]{1,0:T(8,128)} fusion(f32[256,4096]{1,0:T(8,128)} %bitcast.106, f32[3,4096]{1,0:T(4,128)S(1)} %slice.127, f32[4096]{0:T(1024)S(1)} %bitcast.131, f32[4096]{0:T(1024)S(1)} %bitcast.129, f32[4096]{0:T(1024)S(1)} %bitcast.130, f32[4096]{0:T(1024)S(1)} %bitcast.128), kind=kLoop, calls=%fused_computation.30 | loop fusion | flops 14680064 | bytes 8503296 | tf_op jit(solution)/shard_map/jit(silu)/mul | solution.py:28
  101.3 5.6 %copy.57 = f32[256,4096]{0,1:T(8,128)} copy(f32[256,4096]{1,0:T(8,128)} %divide_multiply_fusion) | data formatting | bytes 8388608 | tf_op jit(solution)/shard_map/jit(silu)/mul | solution.py:28
  106.9 7.3 %fusion.28 = f32[4,16,64,128]{3,2,1,0:T(8,128)} fusion(f32[256,4,128,1]{0,2,3,1:T(8,128)S(1)} %bitcast.118, f32[256,4,16,64]{0,3,2,1:T(8,128)} %bitcast.107, f32[256,4,16]{0,2,1:T(8,128)S(1)} %get-tuple-element.33, f32[4,16]{1,0:T(4,128)S(1)} %exponential_multiply_fusion), kind=kOutput, calls=%fused_computation.34 | convolution fusion | flops 1612185600 | bytes 6881536 | tf_op jit(solution)/shard_map/while/body/eval_jaxpr/sgh,sghp,sgn->ghpn/dot_general | solution.py:50
  114.2 1.7 reshape.89
  115.9 6.6 %copy.68 = f32[1,64,8192]{1,0,2:T(1,128)} copy(f32[1,64,8192]{2,1,0:T(8,128)S(1)} %reshape.89) | data formatting | bytes 4194304 | tf_op jit(solution)/shard_map/reshape | solution.py:122
  122.5 0.5 broadcast.41
  123.0 38.3 %reduce.7 = f32[8192,64]{1,0:T(8,128)} reduce(f32[8192,1,64]{2,1,0:T(1,128)} %bitcast.112, f32[]{:T(128)} %broadcast.41), dimensions={1}, to_apply=%bitcast.91.reduce_sub_computation | reduce | bytes 4194308
  161.3 5.5 %reshape.104 = f32[16,1,32768]{2,1,0:T(1,128)} reshape(f32[8192,64]{1,0:T(8,128)} %reduce.7) | data formatting | bytes 4194304
  166.9 7.1 %all-to-all-start.4 = ((f32[16,1,32768]{2,1,0:T(1,128)}), f32[16,1,32768]{2,1,0:T(1,128)}, u32[]{:S(2)}, u32[]{:S(2)}) async-start(f32[16,1,32768]{2,1,0:T(1,128)} %reshape.104), calls=%async_computation.4 | async-start | bytes 4194304 | tf_op jit(solution)/shard_map/all_to_all | solution.py:123
  173.9 0.6 dynamic-slice
  175.3 0.2 dynamic-update-slice
  175.5 62.4 %all-reduce = f32[1024]{0:T(1024)S(1)} all-reduce(f32[1024]{0:T(1024)S(1)} %dynamic-update-slice), channel_id=2, replica_groups=mesh['ctx'=16,'head'=2] {'ctx'}, use_global_device_ids=true, to_apply=%add | all-reduce | flops 1024 | bytes 8192
  238.2 7.2 %reduce.8 = f32[16,32768]{1,0:T(8,128)S(1)} reduce(f32[16,1,32768]{2,1,0:T(1,128)} %all-to-all-done.4, f32[]{:T(128)} %broadcast.41), dimensions={1}, to_apply=%all_to_all.93.reduce_sub_computation | reduce | bytes 4194308 | tf_op jit(solution)/shard_map/all_to_all | solution.py:123
  245.5 6.6 %reshape.105 = f32[8192,1,64]{2,1,0:T(1,128)} reshape(f32[16,32768]{1,0:T(8,128)S(1)} %reduce.8) | data formatting | bytes 4194304
  252.0 3.4 copy.86
  255.4 2.1 fusion.31
  257.5 2.5 copy.72
  260.0 5.9 %all-to-all-start.5 = ((f32[16,64,512]{2,1,0:T(8,128)}), f32[16,64,512]{2,1,0:T(8,128)S(1)}, u32[]{:S(2)}, u32[]{:S(2)}) async-start(f32[16,64,512]{2,1,0:T(8,128)} %copy.72), calls=%async_computation.5 | async-start | bytes 4194304 | tf_op jit(solution)/shard_map/all_to_all | solution.py:133
  266.0 1.1 divide_multiply_fusion.2
  267.1 1.2 copy.58
  268.3 2.0 fusion.66
  270.4 4.9 %fusion.34 = f32[4,16,64,256]{3,2,1,0:T(8,128)} fusion(f32[256,4,128,1]{0,2,3,1:T(8,128)S(1)} %bitcast.116), kind=kOutput, calls=%fused_computation.36 | convolution fusion | flops 1610612736 | bytes 4718592 | tf_op jit(solution)/shard_map/while/body/eval_jaxpr/tgn,ghpn->tghp/dot_general | solution.py:46
  275.3 38.1 %all-to-all-done.5 = f32[16,64,512]{2,1,0:T(8,128)S(1)} async-done(((f32[16,64,512]{2,1,0:T(8,128)}), f32[16,64,512]{2,1,0:T(8,128)S(1)}, u32[]{:S(2)}, u32[]{:S(2)}) %all-to-all-start.5) | async-done | bytes 2097184 | tf_op jit(solution)/shard_map/all_to_all | solution.py:133
  313.4 2.5 copy.73
  315.9 1.6 reshape.91
  317.6 3.4 fusion.67
  321.0 22.4 %multiply_reduce_fusion = (f32[256,4]{0,1:T(4,128)S(1)}, f32[256,4,16,64]{0,3,2,1:T(8,128)}) fusion(f32[4,16,64,256]{3,2,1,0:T(8,128)S(1)} %fusion.67, f32[256,4,16]{0,2,1:T(8,128)S(1)} %get-tuple-element.32, f32[4,16,64,256]{3,2,1,0:T(8,128)} %fusion.34, f32[256,4,16,64]{0,3,2,1:T(8,128)S(1)} %bitcast.108, f32[4,16,256]{2,1,0:T(8,128)S(1)} %get-tuple-element.34, ...), kind=kOutput, calls=%fused_computation.27 | convolution fusion | flops 3244293120 | bytes 18026496 | tf_op jit(solution)/shard_map/while/body/eval_jaxpr/ghts,sghp->tghp/dot_general | solution.py:42
  343.6 0.6 mul.253
  344.2 5.8 %copy.91 = f32[32,8,4,1024]{3,1,2,0:T(8,128)} copy(f32[32,8,4,1024]{3,2,1,0:T(4,128)S(1)} %bitcast.113) | data formatting | bytes 8388608
  349.9 5.6 %copy.76 = f32[256,4096]{1,0:T(8,128)} copy(f32[256,4096]{0,1:T(8,128)} %bitcast.120) | data formatting | bytes 8388608 | tf_op jit(solution)/shard_map/reshape | solution.py:142
  355.6 6.3 %multiply_multiply_fusion = f32[256,4096]{1,0:T(8,128)} fusion(f32[256,4096]{1,0:T(8,128)} %copy.76, f32[256,4096]{1,0:T(8,128)} %bitcast.111, f32[4096]{0:T(1024)S(1)} %copy-done.3), kind=kLoop, calls=%fused_computation.26 | loop fusion | flops 2097152 | bytes 12599296 | tf_op jit(solution)/shard_map/mul | solution.py:144
  (47 shorter events, 2.2 us)
Async XLA Ops:
  1.6 6.3 %all-to-all-start.3 = ((f32[128,2,64]{0,2,1:T(8,128)}), f32[128,2,64]{0,2,1:T(8,128)S(1)}, u32[]{:S(2)}, u32[]{:S(2)}) async-start(f32[128,2,64]{0,2,1:T(8,128)} %bitcast.24), calls=%async_computation.3 | async-start | bytes 131072 | tf_op jit(solution)/shard_map/all_to_all | solution.py:77
  7.8 9.7 %all-to-all-start.1 = ((f32[128,2,512]{0,2,1:T(8,128)}), f32[128,2,512]{0,2,1:T(8,128)S(1)}, u32[]{:S(2)}, u32[]{:S(2)}) async-start(f32[128,2,512]{0,2,1:T(8,128)} %bitcast.4), calls=%async_computation.1 | async-start | bytes 1048576 | tf_op jit(solution)/shard_map/all_to_all | solution.py:75
  17.5 9.1 %all-to-all-start.2 = ((f32[128,2,512]{0,2,1:T(8,128)}), f32[128,2,512]{0,2,1:T(8,128)S(1)}, u32[]{:S(2)}, u32[]{:S(2)}) async-start(f32[128,2,512]{0,2,1:T(8,128)} %bitcast.7), calls=%async_computation.2 | async-start | bytes 1048576 | tf_op jit(solution)/shard_map/all_to_all | solution.py:76
  26.6 5.8 %copy-start.4 = (f32[4,1024]{1,0:T(4,128)S(1)}, f32[4,1024]{1,0:T(4,128)}, u32[]{:S(2)}) copy-start(f32[4,1024]{1,0:T(4,128)} %param.14) | copy-start | bytes 49156
  26.6 5.8 %copy-start.5 = (f32[4,1024]{1,0:T(4,128)S(1)}, f32[4,1024]{1,0:T(4,128)}, u32[]{:S(2)}) copy-start(f32[4,1024]{1,0:T(4,128)} %param.13) | copy-start | bytes 49156
  26.6 5.9 %copy-start.2 = (f32[4,8192]{1,0:T(4,128)S(1)}, f32[4,8192]{1,0:T(4,128)}, u32[]{:S(2)}) copy-start(f32[4,8192]{1,0:T(4,128)} %param.12) | copy-start | bytes 393220
  26.6 49.6 %all-to-all-start = ((f32[128,2,4096]{0,2,1:T(8,128)}), f32[128,2,4096]{0,2,1:T(8,128)}, u32[]{:S(2)}, u32[]{:S(2)}) async-start(f32[128,2,4096]{0,2,1:T(8,128)} %bitcast.110), calls=%async_computation | async-start | bytes 8388608 | tf_op jit(solution)/shard_map/all_to_all | solution.py:74
  82.8 9.0 %collective-permute-start = (f32[3,5120]{1,0:T(4,128)S(1)}, f32[3,5120]{1,0:T(4,128)S(1)}, u32[]{:S(2)}, u32[]{:S(2)}) collective-permute-start(f32[3,5120]{1,0:T(4,128)S(1)} %pad_maximum_fusion.3), channel_id=1, source_target_pairs={{0,2},{2,4},{4,6},{6,8},{8,10},{10,12},{12,14},{14,16},{16,18},{18... | collective-permute-start | bytes 184328 | tf_op jit(solution)/shard_map/ppermute | solution.py:18
  161.3 12.6 %copy-start.6 = (u32[32]{0:T(128)S(1)}, u32[32]{0:T(128)}, u32[]{:S(2)}) copy-start(u32[32]{0:T(128)} %constant.53) | copy-start | bytes 388
  166.9 71.4 %all-to-all-start.4 = ((f32[16,1,32768]{2,1,0:T(1,128)}), f32[16,1,32768]{2,1,0:T(1,128)}, u32[]{:S(2)}, u32[]{:S(2)}) async-start(f32[16,1,32768]{2,1,0:T(1,128)} %reshape.104), calls=%async_computation.4 | async-start | bytes 4194304 | tf_op jit(solution)/shard_map/all_to_all | solution.py:123
  260.0 53.3 %all-to-all-start.5 = ((f32[16,64,512]{2,1,0:T(8,128)}), f32[16,64,512]{2,1,0:T(8,128)S(1)}, u32[]{:S(2)}, u32[]{:S(2)}) async-start(f32[16,64,512]{2,1,0:T(8,128)} %copy.72), calls=%async_computation.5 | async-start | bytes 4194304 | tf_op jit(solution)/shard_map/all_to_all | solution.py:133
  317.6 3.5 copy-start
  317.6 3.5 copy-start.1
  349.9 5.6 %copy-start.3 = (f32[4096]{0:T(1024)S(1)}, f32[4096]{0:T(1024)}, u32[]{:S(2)}) copy-start(f32[4096]{0:T(1024)} %param.15) | copy-start | bytes 49156
where the time goes:
time: 366 us; the launch traced here: 362 us
  waiting for transfers between devices  84.2 us (23%)
  local copies, waits for them, and re-layouts  70.1 us (19%)
  other arithmetic  64.9 us (18%)
  blocking collectives  62.4 us (17%)
  matrix products  42.1 us (12%)
  starting transfers between devices  37.1 us (10%)
    unnamed x1, blocking collectives  62.4 us
    all_to_all x1, waiting for transfers between devices, shards(): lax.all_to_all(moving[0], 'head', split_axis=1, concat_axis=0, tiled=True)  40.1 us
    unnamed x1, other arithmetic  38.3 us
    all_to_all x1, waiting for transfers between devices, shards(): lax.all_to_all(prefix, 'ctx', split_axis=0, concat_axis=2, tiled=True)  38.1 us
    unnamed x25, local copies, waits for them, and re-layouts  30.4 us
    dot_general x1, matrix products, block_pass(): jnp.einsum('ghts,sghp->tghp', scores[:, None] * damping, inputs_act, prec...  22.4 us
    mul x3, other arithmetic, causal_conv(): return jax.nn.silu(summed)  10.3 us
    reshape x2, local copies, waits for them, and re-layouts, shards(): flattened = final_state.reshape(1, local_heads, P_SIZE * N)  8.32 us
  transfers between devices with their start and end apart: 7, of which 5 were waited for; matrix products, arithmetic and copies ran while one was open for 7% of the time, Pallas kernels for 0%

commit v1 on v0

--- a/solution.py
+++ b/solution.py
@@ -10,6 +10,20 @@
 BLOCK = 256
 highest = lax.Precision.HIGHEST
 eps_norm = 1e-05
+
+
+def handle_the_sums_all(x0, join_dim, z_in):
+    after = x0.shape
+    res = x0.reshape(*after[:join_dim], z_in, after[join_dim] // z_in, *after[join_dim + 1 :])
+    r_now = jnp.moveaxis(res, join_dim, 0)
+    return r_now
+
+
+def hubs_post(tile_in, pos_dim):
+    n_now = list(tile_in.shape[1:])
+    n_now[pos_dim] *= tile_in.shape[0]
+    tmp = jnp.moveaxis(tile_in, 0, pos_dim).reshape(n_now)
+    return tmp
 
 
 def passed_along(value, axis, steps):
@@ -130,7 +144,23 @@
     spacing = jnp.where(before, (running - totals)[:, None, :] - running[None, :, :], 0.0)
     weight = jnp.where(before, jnp.exp(spacing), 0.0)
     prefix = jnp.einsum("cdh,dhq->chq", weight, pieces, precision=highest)
-    returned = lax.all_to_all(prefix, "ctx", split_axis=0, concat_axis=2, tiled=True)
+
+    def _form_record(payload, group_axis, load, row_data):
+        inter, tile_out = (lax.axis_size(group_axis), lax.axis_index(group_axis))
+        w2 = handle_the_sums_all(payload, load, inter)
+        wide_out = w2
+        for h in range(1, inter):
+            reply, arr_now = ((tile_out + h) % inter, (tile_out - h) % inter)
+            aux = lax.dynamic_index_in_dim(w2, reply, 0)
+            trail = []
+            for no in range(inter):
+                trail.append((no, (no + h) % inter))
+            known = lax.ppermute(aux, axis_name=group_axis, perm=trail)
+            wide_out = lax.dynamic_update_slice_in_dim(wide_out, known, arr_now, axis=0)
+        arr_next = hubs_post(wide_out, row_data)
+        return arr_next
+
+    returned = _form_record(prefix, "ctx", 0, 2)
     incoming = returned.reshape(groups_here, per_group, P_SIZE, N)
     rising = jnp.exp(jnp.cumsum(decay_groups, 0))
     carried = (

time: 366 us -> 403 us (1.10)
  starting transfers between devices: 37.1 us -> 75.8 us
  waiting for transfers between devices: 84.2 us -> 52 us
  local copies, waits for them, and re-layouts: 70.1 us -> 96 us
  matrix products: 42.1 us -> 47.5 us
    all_to_all x1 -> x0, waiting for transfers between devices: 38.1 us -> none  [shards(): lax.all_to_all(prefix, 'ctx', split_axis=0, concat_axis=2, tiled=True)]
    ppermute x0 -> x15, starting transfers between devices: none -> 30.7 us  [_form_record(): known = lax.ppermute(aux, axis_name=group_axis, perm=trail)]
    dynamic_update_slice x0 -> x15, local copies, waits for them, and re-layouts: none -> 30.3 us  [_form_record(): wide_out = lax.dynamic_update_slice_in_dim(wide_out, known, arr_now, axis=0)]
    all_to_all x1, starting transfers between devices: 7.07 us -> 21.1 us  [shards(): lax.all_to_all(flattened, 'ctx', split_axis=2, concat_axis=0, tiled=True)]
    dot_general x1, matrix products: 3.44 us -> 10.2 us  [shards(): jnp.einsum('tgn,ghpn->tghp', reads_act.reshape(length, groups_here, N), i...]
    ppermute x0 -> x15, waiting for transfers between devices: none -> 6.37 us  [_form_record(): known = lax.ppermute(aux, axis_name=group_axis, perm=trail)]
    all_to_all x1 -> x0, starting transfers between devices: 5.93 us -> none  [shards(): lax.all_to_all(prefix, 'ctx', split_axis=0, concat_axis=2, tiled=True)]
    unnamed x25 -> x57, local copies, waits for them, and re-layouts: 30.4 us -> 28.6 us
  transfers between devices with their start and end apart: 7 -> 21, of which waited for: 5 -> 6; matrix products, arithmetic and copies ran while one was open for 7% -> 18% of each run, Pallas kernels for 0% -> 0%
where the time goes in v1:
time: 403 us; the launch traced here: 396 us
  local copies, waits for them, and re-layouts  96 us (24%)
  starting transfers between devices  75.8 us (19%)
  other arithmetic  61.7 us (15%)
  blocking collectives  61 us (15%)
  waiting for transfers between devices  52 us (13%)
  matrix products  47.5 us (12%)
    unnamed x1, blocking collectives  61 us
    all_to_all x1, waiting for transfers between devices, shards(): lax.all_to_all(moving[0], 'head', split_axis=1, concat_axis=0, tiled=True)  39.5 us
    unnamed x1, other arithmetic  38.4 us
    ppermute x15, starting transfers between devices, _form_record(): known = lax.ppermute(aux, axis_name=group_axis, perm=trail)  30.7 us
    dynamic_update_slice x15, local copies, waits for them, and re-layouts, _form_record(): wide_out = lax.dynamic_update_slice_in_dim(wide_out, known, arr_now, axis=0)  30.3 us
    unnamed x57, local copies, waits for them, and re-layouts  28.6 us
    all_to_all x1, starting transfers between devices, shards(): lax.all_to_all(flattened, 'ctx', split_axis=2, concat_axis=0, tiled=True)  21.1 us
    dot_general x1, matrix products, block_pass(): jnp.einsum('ghts,sghp->tghp', scores[:, None] * damping, inputs_act, prec...  20.1 us
  transfers between devices with their start and end apart: 21, of which 6 were waited for; matrix products, arithmetic and copies ran while one was open for 18% of the time, Pallas kernels for 0%

profile of v1, /device:TPU:11, one launch (start us, length us, event | category | flops | bytes accessed | tf_op | source)
XLA Modules:
  0.0 396.2 jit_solution(7598066878875104426)
XLA Ops:
  1.6 3.3 all-to-all-start.3
  7.8 3.5 all-to-all-start.1
  13.4 4.2 %all-to-all-done.1 = f32[128,2,512]{0,2,1:T(8,128)S(1)} async-done(((f32[128,2,512]{0,2,1:T(8,128)}), f32[128,2,512]{0,2,1:T(8,128)S(1)}, u32[]{:S(2)}, u32[]{:S(2)}) %all-to-all-start.1) | async-done | bytes 524320 | tf_op jit(solution)/shard_map/all_to_all | solution.py:89
  17.6 3.5 all-to-all-start.2
  21.1 5.6 %copy.51 = f32[128,8192]{0,1:T(8,128)} copy(f32[128,8192]{1,0:T(8,128)} %param.8) | data formatting | bytes 8388608 | tf_op args[0]
  26.6 5.7 %all-to-all-start = ((f32[128,2,4096]{0,2,1:T(8,128)}), f32[128,2,4096]{0,2,1:T(8,128)}, u32[]{:S(2)}, u32[]{:S(2)}) async-start(f32[128,2,4096]{0,2,1:T(8,128)} %bitcast.139), calls=%async_computation | async-start | bytes 8388608 | tf_op jit(solution)/shard_map/all_to_all | solution.py:88
  32.9 2.3 reduce-window.12
  36.8 39.5 %all-to-all-done = f32[128,2,4096]{0,2,1:T(8,128)} async-done(((f32[128,2,4096]{0,2,1:T(8,128)}), f32[128,2,4096]{0,2,1:T(8,128)}, u32[]{:S(2)}, u32[]{:S(2)}) %all-to-all-start) | async-done | bytes 4194336 | tf_op jit(solution)/shard_map/all_to_all | solution.py:88
  76.2 5.6 %copy.52 = f32[2,128,4096]{2,1,0:T(8,128)} copy(f32[2,128,4096]{1,2,0:T(8,128)} %bitcast.2) | data formatting | bytes 8388608 | tf_op jit(solution)/shard_map/all_to_all | solution.py:88
  82.8 8.0 %collective-permute-start = (f32[3,5120]{1,0:T(4,128)S(1)}, f32[3,5120]{1,0:T(4,128)S(1)}, u32[]{:S(2)}, u32[]{:S(2)}) collective-permute-start(f32[3,5120]{1,0:T(4,128)S(1)} %pad_maximum_fusion.3), channel_id=1, source_target_pairs={{0,2},{2,4},{4,6},{6,8},{8,10},{10,12},{12,14},{14,16},{16,18},{18... | collective-permute-start | bytes 184328 | tf_op jit(solution)/shard_map/ppermute | solution.py:32
  91.8 8.9 %divide_multiply_fusion = f32[256,4096]{1,0:T(8,128)} fusion(f32[256,4096]{1,0:T(8,128)} %bitcast.135, f32[3,4096]{1,0:T(4,128)S(1)} %slice.127, f32[4096]{0:T(1024)S(1)} %bitcast.159, f32[4096]{0:T(1024)S(1)} %bitcast.157, f32[4096]{0:T(1024)S(1)} %bitcast.158, f32[4096]{0:T(1024)S(1)} %bitcast.156), kind=kLoop, calls=%fused_computation.30 | loop fusion | flops 14680064 | bytes 8503296 | tf_op jit(solution)/shard_map/jit(silu)/mul | solution.py:42
  100.7 5.6 %copy.57 = f32[256,4096]{0,1:T(8,128)} copy(f32[256,4096]{1,0:T(8,128)} %divide_multiply_fusion) | data formatting | bytes 8388608 | tf_op jit(solution)/shard_map/jit(silu)/mul | solution.py:42
  106.9 7.3 %fusion.26 = f32[4,16,64,128]{3,2,1,0:T(8,128)} fusion(f32[256,4,128,1]{0,2,3,1:T(8,128)S(1)} %bitcast.147, f32[256,4,16,64]{0,3,2,1:T(8,128)} %bitcast.136, f32[256,4,16]{0,2,1:T(8,128)S(1)} %get-tuple-element.48, f32[4,16]{1,0:T(4,128)S(1)} %exponential_multiply_fusion), kind=kOutput, calls=%fused_computation.34 | convolution fusion | flops 1612185600 | bytes 6881536 | tf_op jit(solution)/shard_map/while/body/eval_jaxpr/sgh,sghp,sgn->ghpn/dot_general | solution.py:64
  115.9 6.6 %copy.68 = f32[1,64,8192]{1,0,2:T(1,128)} copy(f32[1,64,8192]{2,1,0:T(8,128)S(1)} %reshape.133) | data formatting | bytes 4194304 | tf_op jit(solution)/shard_map/reshape | solution.py:136
  123.0 38.4 %reduce.7 = f32[8192,64]{1,0:T(8,128)} reduce(f32[8192,1,64]{2,1,0:T(1,128)} %bitcast.140, f32[]{:T(128)} %broadcast.71), dimensions={1}, to_apply=%bitcast.118.reduce_sub_computation | reduce | bytes 4194308
  161.3 5.5 %reshape.148 = f32[16,1,32768]{2,1,0:T(1,128)} reshape(f32[8192,64]{1,0:T(8,128)} %reduce.7) | data formatting | bytes 4194304
  166.8 21.1 %all-to-all-start.4 = ((f32[16,1,32768]{2,1,0:T(1,128)}), f32[16,1,32768]{2,1,0:T(1,128)}, u32[]{:S(2)}, u32[]{:S(2)}) async-start(f32[16,1,32768]{2,1,0:T(1,128)} %reshape.148), calls=%async_computation.4 | async-start | bytes 4194304 | tf_op jit(solution)/shard_map/all_to_all | solution.py:137
  190.8 61.0 %all-reduce = f32[1024]{0:T(1024)S(1)} all-reduce(f32[1024]{0:T(1024)S(1)} %dynamic-update-slice), channel_id=2, replica_groups=mesh['ctx'=16,'head'=2] {'ctx'}, use_global_device_ids=true, to_apply=%add | all-reduce | flops 1024 | bytes 8192
  252.7 7.2 %reduce.8 = f32[16,32768]{1,0:T(8,128)S(1)} reduce(f32[16,1,32768]{2,1,0:T(1,128)} %all-to-all-done.4, f32[]{:T(128)} %broadcast.71), dimensions={1}, to_apply=%all_to_all.82.reduce_sub_computation | reduce | bytes 4194308 | tf_op jit(solution)/shard_map/all_to_all | solution.py:137
  259.8 6.6 %reshape.149 = f32[8192,1,64]{2,1,0:T(1,128)} reshape(f32[16,32768]{1,0:T(8,128)S(1)} %reduce.8) | data formatting | bytes 4194304
  266.4 4.2 %copy.84 = f32[1,64,16,512]{3,2,1,0:T(8,128)} copy(f32[1,64,16,512]{1,3,2,0:T(8,128)} %bitcast.138) | data formatting | bytes 4194304 | tf_op jit(solution)/shard_map/all_to_all | solution.py:137
  270.6 3.8 fusion.23
  274.4 2.8 dynamic-slice_bitcast_fusion
  277.2 3.0 collective-permute-start.9
  282.4 2.7 collective-permute-start.6
  286.9 2.1 collective-permute-done.9
  290.3 4.2 %collective-permute-done.8 = f32[1,1,64,512]{3,0,2,1:T(1,128)S(1)} collective-permute-done((f32[1,1,64,512]{3,0,2,1:T(1,128)S(1)}, f32[1,1,64,512]{3,0,2,1:T(1,128)S(1)}, u32[]{:S(2)}, u32[]{:S(2)}) %collective-permute-start.8) | collective-permute-done | bytes 131104 | tf_op jit(solution)/shard_map/ppermute | solution.py:158
  294.5 4.5 %collective-permute-start.3 = (f32[1,1,64,512]{3,0,2,1:T(1,128)S(1)}, f32[1,1,64,512]{3,0,2,1:T(1,128)S(1)}, u32[]{:S(2)}, u32[]{:S(2)}) collective-permute-start(f32[1,1,64,512]{3,0,2,1:T(1,128)S(1)} %get-tuple-element.38), channel_id=1, source_target_pairs={{0,6},{2,8},{4,10},{6,12},{8,14},{10,16},{12,18},{14,20},{16,22},{... | collective-permute-start | bytes 393224 | tf_op jit(solution)/shard_map/ppermute | solution.py:158
  298.9 7.2 %collective-permute-start.2 = (f32[1,1,64,512]{3,0,2,1:T(1,128)S(1)}, f32[1,1,64,512]{3,0,2,1:T(1,128)S(1)}, u32[]{:S(2)}, u32[]{:S(2)}) collective-permute-start(f32[1,1,64,512]{3,0,2,1:T(1,128)S(1)} %get-tuple-element.39), channel_id=1, source_target_pairs={{0,4},{2,6},{4,8},{6,10},{8,12},{10,14},{12,16},{14,18},{16,20},{1... | collective-permute-start | bytes 393224 | tf_op jit(solution)/shard_map/ppermute | solution.py:158
  306.2 3.2 collective-permute-start.1
  309.4 20.1 %fusion = f32[4,16,64,256]{3,2,1,0:T(8,128)} fusion(f32[256,4,16,64]{0,3,2,1:T(8,128)S(1)} %bitcast.137, f32[4,16,256]{2,1,0:T(8,128)S(1)} %copy-done.16, f32[4,256,256]{2,1,0:T(8,128)S(1)} %fusion.61, pred[256,256]{1,0:T(8,128)(4,1)S(1)} %copy-done.17), kind=kOutput, calls=%fused_computation | convolution fusion | flops 3238002688 | bytes 9568256 | tf_op jit(solution)/shard_map/while/body/eval_jaxpr/ghts,sghp->tghp/dot_general | solution.py:56
  331.1 4.4 %collective-permute-start.12 = (f32[1,1,64,512]{3,0,2,1:T(1,128)}, f32[1,1,64,512]{3,0,2,1:T(1,128)}, u32[]{:S(2)}, u32[]{:S(2)}) collective-permute-start(f32[1,1,64,512]{3,0,2,1:T(1,128)} %get-tuple-element.20), channel_id=1, source_target_pairs={{0,24},{2,26},{4,28},{6,30},{8,0},{10,2},{12,4},{14,6},{16,8},{18,... | collective-permute-start | bytes 393224 | tf_op jit(solution)/shard_map/ppermute | solution.py:158
  335.5 5.2 %fusion.29 = f32[4,16,64,256]{3,2,1,0:T(8,128)} fusion(f32[256,4,128,1]{0,2,3,1:T(8,128)S(1)} %bitcast.145), kind=kOutput, calls=%fused_computation.35 | convolution fusion | flops 1610612736 | bytes 4718592 | tf_op jit(solution)/shard_map/while/body/eval_jaxpr/tgn,ghpn->tghp/dot_general | solution.py:60
  340.7 2.3 dynamic_update_slice.48
  343.1 2.3 dynamic_update_slice.49
  345.4 2.3 dynamic_update_slice.50
  347.8 2.3 dynamic_update_slice.51
  350.1 2.3 dynamic_update_slice.52
  352.5 2.3 dynamic_update_slice.53
  359.5 2.3 dynamic_update_slice.58
  361.8 2.3 dynamic_update_slice.59
  364.2 2.3 dynamic_update_slice.60
  366.5 2.3 dynamic_update_slice.61
  368.9 2.3 dynamic_update_slice.62
  372.7 10.2 %multiply_reduce_fusion = (f32[256,4]{0,1:T(4,128)S(1)}, f32[256,4,16,64]{0,3,2,1:T(8,128)}) fusion(f32[4,16,64,128]{3,2,1,0:T(8,128)} %reshape_reshape.3, f32[256,4,128,1]{0,2,3,1:T(8,128)S(1)} %bitcast.146, f32[256,4,16]{0,2,1:T(8,128)S(1)} %get-tuple-element.47, f32[4,16,64,256]{3,2,1,0:T(8,128)} %fusion.29, f32[4,16,64,256]{3,2,1,0:T(8,128)} %fusion), kind=kOutput, calls=%fused_computation.27 | convolution fusion | flops 1616903168 | bytes 15273984 | tf_op jit(solution)/shard_map/tgn,ghpn->tghp/dot_general | solution.py:167
  382.9 5.8 %copy.74 = f32[256,4096]{1,0:T(8,128)} copy(f32[256,4096]{0,1:T(8,128)} %bitcast.143) | data formatting | bytes 8388608 | tf_op jit(solution)/shard_map/reshape | solution.py:172
  389.5 3.9 copy.89
  393.3 2.6 multiply_multiply_fusion
  (121 shorter events, 29.3 us)
Async XLA Ops:
  1.6 6.3 %all-to-all-start.3 = ((f32[128,2,64]{0,2,1:T(8,128)}), f32[128,2,64]{0,2,1:T(8,128)S(1)}, u32[]{:S(2)}, u32[]{:S(2)}) async-start(f32[128,2,64]{0,2,1:T(8,128)} %bitcast.24), calls=%async_computation.3 | async-start | bytes 131072 | tf_op jit(solution)/shard_map/all_to_all | solution.py:91
  7.8 9.7 %all-to-all-start.1 = ((f32[128,2,512]{0,2,1:T(8,128)}), f32[128,2,512]{0,2,1:T(8,128)S(1)}, u32[]{:S(2)}, u32[]{:S(2)}) async-start(f32[128,2,512]{0,2,1:T(8,128)} %bitcast.4), calls=%async_computation.1 | async-start | bytes 1048576 | tf_op jit(solution)/shard_map/all_to_all | solution.py:89
  17.6 9.1 %all-to-all-start.2 = ((f32[128,2,512]{0,2,1:T(8,128)}), f32[128,2,512]{0,2,1:T(8,128)S(1)}, u32[]{:S(2)}, u32[]{:S(2)}) async-start(f32[128,2,512]{0,2,1:T(8,128)} %bitcast.7), calls=%async_computation.2 | async-start | bytes 1048576 | tf_op jit(solution)/shard_map/all_to_all | solution.py:90
  26.6 5.8 %copy-start.20 = (f32[4,1024]{1,0:T(4,128)S(1)}, f32[4,1024]{1,0:T(4,128)}, u32[]{:S(2)}) copy-start(f32[4,1024]{1,0:T(4,128)} %param.14) | copy-start | bytes 49156
  26.6 5.8 %copy-start.21 = (f32[4,1024]{1,0:T(4,128)S(1)}, f32[4,1024]{1,0:T(4,128)}, u32[]{:S(2)}) copy-start(f32[4,1024]{1,0:T(4,128)} %param.13) | copy-start | bytes 49156
  26.6 5.9 %copy-start.18 = (f32[4,8192]{1,0:T(4,128)S(1)}, f32[4,8192]{1,0:T(4,128)}, u32[]{:S(2)}) copy-start(f32[4,8192]{1,0:T(4,128)} %param.12) | copy-start | bytes 393220
  26.6 49.6 %all-to-all-start = ((f32[128,2,4096]{0,2,1:T(8,128)}), f32[128,2,4096]{0,2,1:T(8,128)}, u32[]{:S(2)}, u32[]{:S(2)}) async-start(f32[128,2,4096]{0,2,1:T(8,128)} %bitcast.139), calls=%async_computation | async-start | bytes 8388608 | tf_op jit(solution)/shard_map/all_to_all | solution.py:88
  82.8 9.0 %collective-permute-start = (f32[3,5120]{1,0:T(4,128)S(1)}, f32[3,5120]{1,0:T(4,128)S(1)}, u32[]{:S(2)}, u32[]{:S(2)}) collective-permute-start(f32[3,5120]{1,0:T(4,128)S(1)} %pad_maximum_fusion.3), channel_id=1, source_target_pairs={{0,2},{2,4},{4,6},{6,8},{8,10},{10,12},{12,14},{14,16},{16,18},{18... | collective-permute-start | bytes 184328 | tf_op jit(solution)/shard_map/ppermute | solution.py:32
  161.3 27.2 %copy-start.22 = (u32[32]{0:T(128)S(1)}, u32[32]{0:T(128)}, u32[]{:S(2)}) copy-start(u32[32]{0:T(128)} %constant.276) | copy-start | bytes 388
  166.8 85.8 %all-to-all-start.4 = ((f32[16,1,32768]{2,1,0:T(1,128)}), f32[16,1,32768]{2,1,0:T(1,128)}, u32[]{:S(2)}, u32[]{:S(2)}) async-start(f32[16,1,32768]{2,1,0:T(1,128)} %reshape.148), calls=%async_computation.4 | async-start | bytes 4194304 | tf_op jit(solution)/shard_map/all_to_all | solution.py:137
  270.6 38.8 %copy-start = (f32[256,4096]{0,1:T(8,128)S(1)}, f32[256,4096]{0,1:T(8,128)}, u32[]{:S(2)}) copy-start(f32[256,4096]{0,1:T(8,128)} %copy.57) | copy-start | bytes 12582916
  270.6 38.8 %copy-start.16 = (f32[4,16,256]{2,1,0:T(8,128)S(1)}, f32[4,16,256]{2,1,0:T(8,128)}, u32[]{:S(2)}) copy-start(f32[4,16,256]{2,1,0:T(8,128)} %get-tuple-element.50) | copy-start | bytes 196612
  270.6 38.8 %copy-start.17 = (pred[256,256]{1,0:T(8,128)(4,1)S(1)}, pred[256,256]{1,0:T(8,128)(4,1)}, u32[]{:S(2)}) copy-start(pred[256,256]{1,0:T(8,128)(4,1)} %iota_compare_fusion) | copy-start | bytes 196612
  277.1 8.9 %collective-permute-start.10 = (f32[1,1,64,512]{3,0,2,1:T(1,128)S(1)}, f32[1,1,64,512]{3,0,2,1:T(1,128)S(1)}, u32[]{:S(2)}, u32[]{:S(2)}) collective-permute-start(f32[1,1,64,512]{3,0,2,1:T(1,128)S(1)} %get-tuple-element.30), channel_id=1, source_target_pairs={{0,20},{2,22},{4,24},{6,26},{8,28},{10,30},{12,0},{14,2},{16,4},{1... | collective-permute-start | bytes 393224 | tf_op jit(solution)/shard_map/ppermute | solution.py:158
  277.2 11.8 %collective-permute-start.9 = (f32[1,1,64,512]{3,0,2,1:T(1,128)S(1)}, f32[1,1,64,512]{3,0,2,1:T(1,128)S(1)}, u32[]{:S(2)}, u32[]{:S(2)}) collective-permute-start(f32[1,1,64,512]{3,0,2,1:T(1,128)S(1)} %get-tuple-element.32), channel_id=1, source_target_pairs={{0,18},{2,20},{4,22},{6,24},{8,26},{10,28},{12,30},{14,0},{16,2},{... | collective-permute-start | bytes 393224 | tf_op jit(solution)/shard_map/ppermute | solution.py:158
  280.1 14.3 %collective-permute-start.8 = (f32[1,1,64,512]{3,0,2,1:T(1,128)S(1)}, f32[1,1,64,512]{3,0,2,1:T(1,128)S(1)}, u32[]{:S(2)}, u32[]{:S(2)}) collective-permute-start(f32[1,1,64,512]{3,0,2,1:T(1,128)S(1)} %get-tuple-element.33), channel_id=1, source_target_pairs={{0,16},{2,18},{4,20},{6,22},{8,24},{10,26},{12,28},{14,30},{16,0},... | collective-permute-start | bytes 393224 | tf_op jit(solution)/shard_map/ppermute | solution.py:158
  281.5 17.4 %collective-permute-start.7 = (f32[1,1,64,512]{3,0,2,1:T(1,128)S(1)}, f32[1,1,64,512]{3,0,2,1:T(1,128)S(1)}, u32[]{:S(2)}, u32[]{:S(2)}) collective-permute-start(f32[1,1,64,512]{3,0,2,1:T(1,128)S(1)} %get-tuple-element.34), channel_id=1, source_target_pairs={{0,14},{2,16},{4,18},{6,20},{8,22},{10,24},{12,26},{14,28},{16,30}... | collective-permute-start | bytes 393224 | tf_op jit(solution)/shard_map/ppermute | solution.py:158
  282.4 23.8 %collective-permute-start.6 = (f32[1,1,64,512]{3,0,2,1:T(1,128)S(1)}, f32[1,1,64,512]{3,0,2,1:T(1,128)S(1)}, u32[]{:S(2)}, u32[]{:S(2)}) collective-permute-start(f32[1,1,64,512]{3,0,2,1:T(1,128)S(1)} %get-tuple-element.35), channel_id=1, source_target_pairs={{0,12},{2,14},{4,16},{6,18},{8,20},{10,22},{12,24},{14,26},{16,28}... | collective-permute-start | bytes 393224 | tf_op jit(solution)/shard_map/ppermute | solution.py:158
  286.1 43.4 %copy-start.2 = (f32[1,1,64,512]{3,0,2,1:T(1,128)}, f32[1,1,64,512]{3,0,2,1:T(1,128)S(1)}, u32[]{:S(2)}) copy-start(f32[1,1,64,512]{3,0,2,1:T(1,128)S(1)} %collective-permute-done.10) | copy-start | bytes 393220
  286.1 43.5 %collective-permute-start.5 = (f32[1,1,64,512]{3,0,2,1:T(1,128)S(1)}, f32[1,1,64,512]{3,0,2,1:T(1,128)S(1)}, u32[]{:S(2)}, u32[]{:S(2)}) collective-permute-start(f32[1,1,64,512]{3,0,2,1:T(1,128)S(1)} %get-tuple-element.36), channel_id=1, source_target_pairs={{0,10},{2,12},{4,14},{6,16},{8,18},{10,20},{12,22},{14,24},{16,26}... | collective-permute-start | bytes 393224 | tf_op jit(solution)/shard_map/ppermute | solution.py:158
  289.0 40.6 %copy-start.4 = (f32[1,1,64,512]{3,0,2,1:T(1,128)}, f32[1,1,64,512]{3,0,2,1:T(1,128)S(1)}, u32[]{:S(2)}) copy-start(f32[1,1,64,512]{3,0,2,1:T(1,128)S(1)} %collective-permute-done.9) | copy-start | bytes 393220
  289.0 40.7 %collective-permute-start.4 = (f32[1,1,64,512]{3,0,2,1:T(1,128)S(1)}, f32[1,1,64,512]{3,0,2,1:T(1,128)S(1)}, u32[]{:S(2)}, u32[]{:S(2)}) collective-permute-start(f32[1,1,64,512]{3,0,2,1:T(1,128)S(1)} %get-tuple-element.37), channel_id=1, source_target_pairs={{0,8},{2,10},{4,12},{6,14},{8,16},{10,18},{12,20},{14,22},{16,24},... | collective-permute-start | bytes 393224 | tf_op jit(solution)/shard_map/ppermute | solution.py:158
  294.5 35.1 %copy-start.6 = (f32[1,1,64,512]{3,0,2,1:T(1,128)}, f32[1,1,64,512]{3,0,2,1:T(1,128)S(1)}, u32[]{:S(2)}) copy-start(f32[1,1,64,512]{3,0,2,1:T(1,128)S(1)} %collective-permute-done.8) | copy-start | bytes 393220
  294.5 35.3 %collective-permute-start.3 = (f32[1,1,64,512]{3,0,2,1:T(1,128)S(1)}, f32[1,1,64,512]{3,0,2,1:T(1,128)S(1)}, u32[]{:S(2)}, u32[]{:S(2)}) collective-permute-start(f32[1,1,64,512]{3,0,2,1:T(1,128)S(1)} %get-tuple-element.38), channel_id=1, source_target_pairs={{0,6},{2,8},{4,10},{6,12},{8,14},{10,16},{12,18},{14,20},{16,22},{... | collective-permute-start | bytes 393224 | tf_op jit(solution)/shard_map/ppermute | solution.py:158
  298.9 30.6 %copy-start.8 = (f32[1,1,64,512]{3,0,2,1:T(1,128)}, f32[1,1,64,512]{3,0,2,1:T(1,128)S(1)}, u32[]{:S(2)}) copy-start(f32[1,1,64,512]{3,0,2,1:T(1,128)S(1)} %collective-permute-done.7) | copy-start | bytes 393220
  298.9 32.1 %collective-permute-start.2 = (f32[1,1,64,512]{3,0,2,1:T(1,128)S(1)}, f32[1,1,64,512]{3,0,2,1:T(1,128)S(1)}, u32[]{:S(2)}, u32[]{:S(2)}) collective-permute-start(f32[1,1,64,512]{3,0,2,1:T(1,128)S(1)} %get-tuple-element.39), channel_id=1, source_target_pairs={{0,4},{2,6},{4,8},{6,10},{8,12},{10,14},{12,16},{14,18},{16,20},{1... | collective-permute-start | bytes 393224 | tf_op jit(solution)/shard_map/ppermute | solution.py:158
  306.2 23.4 %copy-start.10 = (f32[1,1,64,512]{3,0,2,1:T(1,128)}, f32[1,1,64,512]{3,0,2,1:T(1,128)S(1)}, u32[]{:S(2)}) copy-start(f32[1,1,64,512]{3,0,2,1:T(1,128)S(1)} %collective-permute-done.6) | copy-start | bytes 393220
  306.2 29.3 %collective-permute-start.1 = (f32[1,1,64,512]{3,0,2,1:T(1,128)S(1)}, f32[1,1,64,512]{3,0,2,1:T(1,128)S(1)}, u32[]{:S(2)}, u32[]{:S(2)}) collective-permute-start(f32[1,1,64,512]{3,0,2,1:T(1,128)S(1)} %get-tuple-element.40), channel_id=1, source_target_pairs={{0,2},{2,4},{4,6},{6,8},{8,10},{10,12},{12,14},{14,16},{16,18},{18... | collective-permute-start | bytes 393224 | tf_op jit(solution)/shard_map/ppermute | solution.py:158
  329.6 11.1 %copy-start.11 = (f32[1,1,64,512]{3,0,2,1:T(1,128)}, f32[1,1,64,512]{3,0,2,1:T(1,128)S(1)}, u32[]{:S(2)}) copy-start(f32[1,1,64,512]{3,0,2,1:T(1,128)S(1)} %collective-permute-done.5) | copy-start | bytes 393220
  329.6 25.2 %copy-start.9 = (f32[1,1,64,512]{3,0,2,1:T(1,128)S(1)}, f32[1,1,64,512]{3,0,2,1:T(1,128)}, u32[]{:S(2)}) copy-start(f32[1,1,64,512]{3,0,2,1:T(1,128)} %copy-done.8) | copy-start | bytes 393220
  329.6 26.4 %copy-start.7 = (f32[1,1,64,512]{3,0,2,1:T(1,128)S(1)}, f32[1,1,64,512]{3,0,2,1:T(1,128)}, u32[]{:S(2)}) copy-start(f32[1,1,64,512]{3,0,2,1:T(1,128)} %copy-done.6) | copy-start | bytes 393220
  329.6 27.5 %copy-start.5 = (f32[1,1,64,512]{3,0,2,1:T(1,128)S(1)}, f32[1,1,64,512]{3,0,2,1:T(1,128)}, u32[]{:S(2)}) copy-start(f32[1,1,64,512]{3,0,2,1:T(1,128)} %copy-done.4) | copy-start | bytes 393220
  329.6 28.7 %copy-start.3 = (f32[1,1,64,512]{3,0,2,1:T(1,128)S(1)}, f32[1,1,64,512]{3,0,2,1:T(1,128)}, u32[]{:S(2)}) copy-start(f32[1,1,64,512]{3,0,2,1:T(1,128)} %copy-done.2) | copy-start | bytes 393220
  329.6 39.2 %collective-permute-start.15 = (f32[1,1,64,512]{3,0,2,1:T(1,128)S(1)}, f32[1,1,64,512]{3,0,2,1:T(1,128)}, u32[]{:S(2)}, u32[]{:S(2)}) collective-permute-start(f32[1,1,64,512]{3,0,2,1:T(1,128)S(1)} %get-tuple-element.17), channel_id=1, source_target_pairs={{0,30},{2,0},{4,2},{6,4},{8,6},{10,8},{12,10},{14,12},{16,14},{18,... | collective-permute-start | bytes 393224 | tf_op jit(solution)/shard_map/ppermute | solution.py:158
  329.7 11.0 %copy-start.12 = (f32[1,1,64,512]{3,0,2,1:T(1,128)}, f32[1,1,64,512]{3,0,2,1:T(1,128)S(1)}, u32[]{:S(2)}) copy-start(f32[1,1,64,512]{3,0,2,1:T(1,128)S(1)} %collective-permute-done.4) | copy-start | bytes 393220
  329.7 36.8 %collective-permute-start.14 = (f32[1,1,64,512]{3,0,2,1:T(1,128)S(1)}, f32[1,1,64,512]{3,0,2,1:T(1,128)}, u32[]{:S(2)}, u32[]{:S(2)}) collective-permute-start(f32[1,1,64,512]{3,0,2,1:T(1,128)S(1)} %get-tuple-element.18), channel_id=1, source_target_pairs={{0,28},{2,30},{4,0},{6,2},{8,4},{10,6},{12,8},{14,10},{16,12},{18,... | collective-permute-start | bytes 393224 | tf_op jit(solution)/shard_map/ppermute | solution.py:158
  329.8 10.9 %copy-start.13 = (f32[1,1,64,512]{3,0,2,1:T(1,128)}, f32[1,1,64,512]{3,0,2,1:T(1,128)S(1)}, u32[]{:S(2)}) copy-start(f32[1,1,64,512]{3,0,2,1:T(1,128)S(1)} %collective-permute-done.3) | copy-start | bytes 393220
  329.8 34.4 %collective-permute-start.13 = (f32[1,1,64,512]{3,0,2,1:T(1,128)}, f32[1,1,64,512]{3,0,2,1:T(1,128)}, u32[]{:S(2)}, u32[]{:S(2)}) collective-permute-start(f32[1,1,64,512]{3,0,2,1:T(1,128)} %get-tuple-element.19), channel_id=1, source_target_pairs={{0,26},{2,28},{4,30},{6,0},{8,2},{10,4},{12,6},{14,8},{16,10},{18,... | collective-permute-start | bytes 393224 | tf_op jit(solution)/shard_map/ppermute | solution.py:158
  331.1 9.6 %copy-start.14 = (f32[1,1,64,512]{3,0,2,1:T(1,128)}, f32[1,1,64,512]{3,0,2,1:T(1,128)S(1)}, u32[]{:S(2)}) copy-start(f32[1,1,64,512]{3,0,2,1:T(1,128)S(1)} %collective-permute-done.2) | copy-start | bytes 393220
  331.1 30.7 %collective-permute-start.12 = (f32[1,1,64,512]{3,0,2,1:T(1,128)}, f32[1,1,64,512]{3,0,2,1:T(1,128)}, u32[]{:S(2)}, u32[]{:S(2)}) collective-permute-start(f32[1,1,64,512]{3,0,2,1:T(1,128)} %get-tuple-element.20), channel_id=1, source_target_pairs={{0,24},{2,26},{4,28},{6,30},{8,0},{10,2},{12,4},{14,6},{16,8},{18,... | collective-permute-start | bytes 393224 | tf_op jit(solution)/shard_map/ppermute | solution.py:158
  335.5 5.2 %copy-start.15 = (f32[1,1,64,512]{3,0,2,1:T(1,128)}, f32[1,1,64,512]{3,0,2,1:T(1,128)S(1)}, u32[]{:S(2)}) copy-start(f32[1,1,64,512]{3,0,2,1:T(1,128)S(1)} %collective-permute-done.1) | copy-start | bytes 393220
  335.5 24.0 %collective-permute-start.11 = (f32[1,1,64,512]{3,0,2,1:T(1,128)}, f32[1,1,64,512]{3,0,2,1:T(1,128)}, u32[]{:S(2)}, u32[]{:S(2)}) collective-permute-start(f32[1,1,64,512]{3,0,2,1:T(1,128)} %get-tuple-element.28), channel_id=1, source_target_pairs={{0,22},{2,24},{4,26},{6,28},{8,30},{10,0},{12,2},{14,4},{16,6},{18... | collective-permute-start | bytes 393224 | tf_op jit(solution)/shard_map/ppermute | solution.py:158
  389.4 3.9 copy-start.1
  389.4 3.9 copy-start.19
